TPU v7x, 512 devices: a whole 4x8x8 slice. The times are simulated.
512 devices in a mesh: energy: 32 (over x, z_hi, core), cuts: 16 (over z_lo, y).
Axes of the slice: x: 4, y: 8, z: 8 (z_hi: 4, z_lo: 2; z = z_hi * 2 + z_lo), core: 2. Of those that a mesh axis runs over, the one named last changes fastest.
Arguments:
- green_diag: bfloat16 [16, 128, 2, 256, 256], P('cuts', 'energy'), may hold values from -0.375 to 0.375
- green_upper: bfloat16 [16, 128, 2, 256, 256], P('cuts', 'energy'), may hold values from -0.375 to 0.375
- sigma_lesser: bfloat16 [16, 128, 2, 256, 256], P('cuts', 'energy'), may hold values from -6 to 6
- screening: bfloat16 [16, 128, 2, 256, 256], P('cuts', 'energy'), may hold values from -0.375 to 0.375
Outputs:
- polar_screened: bfloat16 [16, 128, 2, 256, 256], P('cuts', 'energy')
All inputs are finite; a program needn't handle non-finite values.
Results may differ from a plain program's by a relative error of at most 0.013.
Values may be sent and summed in bfloat16 or wider, within the bound.
No kernel may reach another device: no remote copies, remote signals or barrier semaphores. Data moves between devices by JAX's collectives and lax.ppermute only.
A program may use at most 64 MiB of HBM per device.

v0:
```python
import math
import jax
import jax.numpy as jnp
from jax import lax
from jax.sharding import PartitionSpec as P


def shifted(value, axis, steps):
    count = lax.axis_size(axis)
    leading, last = (max(0, -steps), min(count, count - steps))
    return lax.ppermute(value, axis, [(source, source + steps) for source in range(leading, last)])


def times_block(left, right):
    real = jnp.einsum(
        "eij,ejk->eik", left[:, 0], right[:, 0], preferred_element_type=jnp.float32
    ) - jnp.einsum("eij,ejk->eik", left[:, 1], right[:, 1], preferred_element_type=jnp.float32)
    imag = jnp.einsum(
        "eij,ejk->eik", left[:, 0], right[:, 1], preferred_element_type=jnp.float32
    ) + jnp.einsum("eij,ejk->eik", left[:, 1], right[:, 0], preferred_element_type=jnp.float32)
    return jnp.stack([real, imag], axis=1)


def times_adjoint(left, right):
    real = jnp.einsum(
        "eij,ekj->eik", left[:, 0], right[:, 0], preferred_element_type=jnp.float32
    ) + jnp.einsum("eij,ekj->eik", left[:, 1], right[:, 1], preferred_element_type=jnp.float32)
    imag = jnp.einsum(
        "eij,ekj->eik", left[:, 1], right[:, 0], preferred_element_type=jnp.float32
    ) - jnp.einsum("eij,ekj->eik", left[:, 0], right[:, 1], preferred_element_type=jnp.float32)
    return jnp.stack([real, imag], axis=1)


def angle_table(rows_count, cols_count, period):
    row_index = lax.broadcasted_iota(jnp.int32, (rows_count, cols_count), 0)
    col_index = lax.broadcasted_iota(jnp.int32, (rows_count, cols_count), 1)
    phase = (row_index * col_index % period).astype(jnp.float32)
    return phase * (2.0 * math.pi / period)


def split_table_dot(table, data):
    upper = table.astype(jnp.bfloat16)
    lower = (table - upper.astype(jnp.float32)).astype(jnp.bfloat16)
    return jnp.dot(upper, data, preferred_element_type=jnp.float32) + jnp.dot(
        lower, data, preferred_element_type=jnp.float32
    )


def correlate(spread):
    energies = spread.shape[0]
    period = 2 * energies
    forward = angle_table(period, energies, period)
    inverse = angle_table(energies, period, period)
    cos_inv = jnp.cos(inverse)
    sin_inv = jnp.sin(inverse)
    real_part = spread[:, 0].reshape(energies, -1)
    imag_part = spread[:, 1].reshape(energies, -1)
    width = real_part.shape[1]
    joined = jnp.concatenate([real_part, imag_part], axis=1)
    cos_both = split_table_dot(jnp.cos(forward), joined)
    sin_both = split_table_dot(jnp.sin(forward), joined)
    spec_real = cos_both[:, :width] + sin_both[:, width:]
    spec_imag = cos_both[:, width:] - sin_both[:, :width]
    power = spec_real * spec_real + spec_imag * spec_imag
    lag_real = jnp.dot(cos_inv, power) / period
    lag_imag = jnp.dot(sin_inv, power) / period
    polar = jnp.stack([lag_real, lag_imag], axis=1) / energies
    return polar.reshape(spread.shape).astype(jnp.bfloat16)


def shards(green_diag, green_upper, sigma_lesser, screening):
    sigma_next = shifted(sigma_lesser, "cuts", -1)
    own_term = times_block(green_diag[0], sigma_lesser[0]).astype(jnp.bfloat16)
    pair_term = times_block(green_upper[0], sigma_next[0]).astype(jnp.bfloat16)
    lesser = (
        times_adjoint(own_term, green_diag[0]) + times_adjoint(pair_term, green_upper[0])
    ).astype(jnp.bfloat16)
    entries = lax.all_to_all(lesser, "energy", split_axis=2, concat_axis=0, tiled=True)
    polar_rows = correlate(entries)
    back_field = lax.all_to_all(polar_rows, "energy", split_axis=0, concat_axis=2, tiled=True)
    screened_left = times_block(screening[0], back_field).astype(jnp.bfloat16)
    result_field = times_adjoint(screened_left, screening[0]).astype(jnp.bfloat16)
    return result_field[None]


def solution(mesh):
    in_specs = (
        P("cuts", "energy", None, None, None),
        P("cuts", "energy", None, None, None),
        P("cuts", "energy", None, None, None),
        P("cuts", "energy", None, None, None),
    )
    out_specs = P("cuts", "energy", None, None, None)
    return jax.shard_map(shards, mesh=mesh, in_specs=in_specs, out_specs=out_specs, check_vma=False)
```

profile of v0, /device:TPU:57, one launch (start us, length us, event | category | flops | bytes accessed | tf_op | source)
XLA Modules:
  0.0 122.9 jit_solution(17262940203430919250)
XLA Ops:
  0.0 1.4 %copy.101 = bf16[1,4,2,256,256]{4,3,1,2,0:T(8,128)(2,1)S(1)} copy(bf16[1,4,2,256,256]{4,3,2,1,0:T(8,128)(2,1)} %param.6) | data formatting | bytes 2097152 | tf_op args[2]
  1.4 3.0 %collective-permute-start = (bf16[1,4,2,256,256]{4,3,1,2,0:T(8,128)(2,1)S(1)}, bf16[1,4,2,256,256]{4,3,1,2,0:T(8,128)(2,1)S(1)}, u32[]{:S(2)}, u32[]{:S(2)}) collective-permute-start(bf16[1,4,2,256,256]{4,3,1,2,0:T(8,128)(2,1)S(1)} %copy.101), channel_id=1, source_target_pairs={{1,0},{2,1},{3,2},{4,3},{5,4},{6,5},{7,6},{8,7},{9,8},{10,9},{11,1... | collective-permute-start | bytes 3145736 | tf_op jit(solution)/shard_map/ppermute | solution.py:11
  5.4 0.3 fusion.26
  5.7 0.6 copy-done.1
  6.7 0.3 fusion.8
  7.7 21.7 %collective-permute-done = bf16[1,4,2,256,256]{4,3,1,2,0:T(8,128)(2,1)S(1)} collective-permute-done((bf16[1,4,2,256,256]{4,3,1,2,0:T(8,128)(2,1)S(1)}, bf16[1,4,2,256,256]{4,3,1,2,0:T(8,128)(2,1)S(1)}, u32[]{:S(2)}, u32[]{:S(2)}) %collective-permute-start) | collective-permute-done | bytes 1048608 | tf_op jit(solution)/shard_map/ppermute | solution.py:11
  30.4 0.3 fusion.28
  31.3 0.3 fusion.6
  32.0 0.4 fusion.3
  32.5 0.8 copy.65
  33.3 42.2 %all_to_all.36 = bf16[4,2,256,256]{3,0,1,2:T(4,128)(2,1)S(1)} all-to-all(bf16[4,2,256,256]{3,0,1,2:T(4,128)(2,1)S(1)} %copy.65), channel_id=1, replica_groups=mesh['energy'=32,'cuts'=16] {'energy'}, dimensions={2} | all-to-all | bytes 2097152 | tf_op jit(solution)/shard_map/all_to_all | solution.py:78
  76.3 1.1 fusion.55
  77.4 1.1 fusion.52
  78.5 1.1 convolution_add_fusion.1
  79.7 1.1 convolution_add_fusion
  80.8 0.9 fusion.1
  81.7 0.8 convolution_multiply_fusion.1
  82.5 0.8 convolution_multiply_fusion
  83.3 0.3 copy.87
  83.6 0.3 copy.88
  84.0 1.2 fusion.4
  85.1 4.9 %all-to-all-start.1 = ((bf16[128,2,8,256]{3,2,1,0:T(8,128)(2,1)}), bf16[128,2,8,256]{3,2,1,0:T(8,128)(2,1)S(1)}, u32[]{:S(2)}, u32[]{:S(2)}) async-start(bf16[128,2,8,256]{3,2,1,0:T(8,128)(2,1)} %fusion.4), calls=%async_computation.1 | async-start | bytes 2097152 | tf_op jit(solution)/shard_map/all_to_all | solution.py:80
  90.2 28.7 %all-to-all-done.1 = bf16[128,2,8,256]{3,2,1,0:T(8,128)(2,1)S(1)} async-done(((bf16[128,2,8,256]{3,2,1,0:T(8,128)(2,1)}), bf16[128,2,8,256]{3,2,1,0:T(8,128)(2,1)S(1)}, u32[]{:S(2)}, u32[]{:S(2)}) %all-to-all-start.1) | async-done | bytes 1048608 | tf_op jit(solution)/shard_map/all_to_all | solution.py:80
  118.9 0.4 fusion.23
  119.3 0.3 fusion.24
  119.6 0.3 fusion.13
  120.0 0.3 fusion.30
  120.3 0.4 fusion.14
  120.7 0.3 fusion.29
  121.0 0.3 fusion.18
  121.4 0.3 fusion.17
  121.9 1.0 copy.78
  (29 shorter events, 4.8 us)
Async XLA Ops:
  0.0 4.4 %copy-start = (bf16[1,4,2,256,256]{4,3,2,1,0:T(8,128)(2,1)S(1)}, bf16[1,4,2,256,256]{4,3,2,1,0:T(8,128)(2,1)}, u32[]{:S(2)}) copy-start(bf16[1,4,2,256,256]{4,3,2,1,0:T(8,128)(2,1)} %param.4) | copy-start | bytes 3145732
  1.4 28.0 %collective-permute-start = (bf16[1,4,2,256,256]{4,3,1,2,0:T(8,128)(2,1)S(1)}, bf16[1,4,2,256,256]{4,3,1,2,0:T(8,128)(2,1)S(1)}, u32[]{:S(2)}, u32[]{:S(2)}) collective-permute-start(bf16[1,4,2,256,256]{4,3,1,2,0:T(8,128)(2,1)S(1)} %copy.101), channel_id=1, source_target_pairs={{1,0},{2,1},{3,2},{4,3},{5,4},{6,5},{7,6},{8,7},{9,8},{10,9},{11,1... | collective-permute-start | bytes 3145736 | tf_op jit(solution)/shard_map/ppermute | solution.py:11
  5.1 1.2 copy-start.1
  84.0 6.1 %copy-start.2 = (bf16[1,4,2,256,256]{4,3,2,1,0:T(8,128)(2,1)S(1)}, bf16[1,4,2,256,256]{4,3,2,1,0:T(8,128)(2,1)}, u32[]{:S(2)}) copy-start(bf16[1,4,2,256,256]{4,3,2,1,0:T(8,128)(2,1)} %param.7) | copy-start | bytes 3145732
  85.1 33.7 %all-to-all-start.1 = ((bf16[128,2,8,256]{3,2,1,0:T(8,128)(2,1)}), bf16[128,2,8,256]{3,2,1,0:T(8,128)(2,1)S(1)}, u32[]{:S(2)}, u32[]{:S(2)}) async-start(bf16[128,2,8,256]{3,2,1,0:T(8,128)(2,1)} %fusion.4), calls=%async_computation.1 | async-start | bytes 2097152 | tf_op jit(solution)/shard_map/all_to_all | solution.py:80
where the time goes:
time: 123 us
  waiting for transfers between devices  50.4 us (41%)
  blocking collectives  42.2 us (34%)
  matrix products  13.9 us (11%)
  starting transfers between devices  7.91 us (6%)
  local copies, waits for them, and re-layouts  5.47 us (4%)
  other arithmetic  2.62 us (2%)
    all_to_all x1, blocking collectives, shards(): lax.all_to_all(lesser, 'energy', split_axis=2, concat_axis=0, tiled=True)  42.2 us
    all_to_all x1, waiting for transfers between devices, shards(): lax.all_to_all(polar_rows, 'energy', split_axis=0, concat_axis=2, tiled=T...  28.7 us
    ppermute x1, waiting for transfers between devices, shifted(): lax.ppermute(value, axis, [(source, source + steps) for source in range(l...  21.7 us
    all_to_all x1, starting transfers between devices, shards(): lax.all_to_all(polar_rows, 'energy', split_axis=0, concat_axis=2, tiled=T...  4.93 us
    unnamed x15, local copies, waits for them, and re-layouts  3.11 us
    ppermute x1, starting transfers between devices, shifted(): lax.ppermute(value, axis, [(source, source + steps) for source in range(l...  2.98 us
  transfers between devices with their start and end apart: 2, of which 2 were waited for; matrix products, arithmetic and copies ran while one was open for 2% of the time, Pallas kernels for 0%

commit v1 on v0

--- a/solution.py
+++ b/solution.py
@@ -75,7 +75,12 @@
     lesser = (
         times_adjoint(own_term, green_diag[0]) + times_adjoint(pair_term, green_upper[0])
     ).astype(jnp.bfloat16)
-    entries = lax.all_to_all(lesser, "energy", split_axis=2, concat_axis=0, tiled=True)
+    entries = jnp.concatenate(
+        lax.all_to_all(
+            jnp.stack(jnp.split(lesser, lax.axis_size("energy"), axis=2)), "energy", 0, 0
+        ),
+        axis=0,
+    )
     polar_rows = correlate(entries)
     back_field = lax.all_to_all(polar_rows, "energy", split_axis=0, concat_axis=2, tiled=True)
     screened_left = times_block(screening[0], back_field).astype(jnp.bfloat16)

time: 123 us -> 123 us (level)
    unnamed x15 -> x46, local copies, waits for them, and re-layouts: 3.11 us -> 3.33 us
where the time goes in v1:
time: 123 us; the launch traced here: 122 us
  waiting for transfers between devices  50.5 us (41%)
  blocking collectives  42.2 us (34%)
  matrix products  13.8 us (11%)
  starting transfers between devices  7.9 us (6%)
  local copies, waits for them, and re-layouts  4.64 us (4%)
  other arithmetic  2.62 us (2%)
    all_to_all x1, blocking collectives, shards(): lax.all_to_all(jnp.stack(jnp.split(lesser, lax.axis_size('energy'), axis=...  42.2 us
    all_to_all x1, waiting for transfers between devices, shards(): lax.all_to_all(polar_rows, 'energy', split_axis=0, concat_axis=2, tiled=T...  28.7 us
    ppermute x1, waiting for transfers between devices, shifted(): lax.ppermute(value, axis, [(source, source + steps) for source in range(l...  21.7 us
    all_to_all x1, starting transfers between devices, shards(): lax.all_to_all(polar_rows, 'energy', split_axis=0, concat_axis=2, tiled=T...  4.92 us
    unnamed x46, local copies, waits for them, and re-layouts  3.33 us
    ppermute x1, starting transfers between devices, shifted(): lax.ppermute(value, axis, [(source, source + steps) for source in range(l...  2.98 us
  transfers between devices with their start and end apart: 2, of which 2 were waited for; matrix products, arithmetic and copies ran while one was open for 2% of the time, Pallas kernels for 0%

profile of v1, /device:TPU:57, one launch (start us, length us, event | category | flops | bytes accessed | tf_op | source)
XLA Modules:
  0.0 122.3 jit_solution(18437387593843449315)
XLA Ops:
  0.0 1.4 %copy.65 = bf16[1,4,2,256,256]{4,3,1,2,0:T(8,128)(2,1)S(1)} copy(bf16[1,4,2,256,256]{4,3,2,1,0:T(8,128)(2,1)} %param.6) | data formatting | bytes 2097152 | tf_op args[2]
  1.4 3.0 %collective-permute-start = (bf16[1,4,2,256,256]{4,3,1,2,0:T(8,128)(2,1)S(1)}, bf16[1,4,2,256,256]{4,3,1,2,0:T(8,128)(2,1)S(1)}, u32[]{:S(2)}, u32[]{:S(2)}) collective-permute-start(bf16[1,4,2,256,256]{4,3,1,2,0:T(8,128)(2,1)S(1)} %copy.65), channel_id=1, source_target_pairs={{1,0},{2,1},{3,2},{4,3},{5,4},{6,5},{7,6},{8,7},{9,8},{10,9},{11,1... | collective-permute-start | bytes 3145736 | tf_op jit(solution)/shard_map/ppermute | solution.py:11
  5.4 0.3 fusion.26
  5.7 0.6 copy-done.1
  6.7 0.3 fusion.8
  7.4 0.3 fusion.7
  7.7 21.7 %collective-permute-done = bf16[1,4,2,256,256]{4,3,1,2,0:T(8,128)(2,1)S(1)} collective-permute-done((bf16[1,4,2,256,256]{4,3,1,2,0:T(8,128)(2,1)S(1)}, bf16[1,4,2,256,256]{4,3,1,2,0:T(8,128)(2,1)S(1)}, u32[]{:S(2)}, u32[]{:S(2)}) %collective-permute-start) | collective-permute-done | bytes 1048608 | tf_op jit(solution)/shard_map/ppermute | solution.py:11
  30.4 0.3 fusion.28
  31.3 0.3 fusion.6
  32.0 0.4 fusion.3
  32.9 42.2 %all_to_all.23 = bf16[32,4,2,8,256]{4,3,1,2,0:T(8,128)(2,1)S(1)} all-to-all(bf16[32,4,2,8,256]{4,3,1,2,0:T(8,128)(2,1)S(1)} %constant_dynamic-update-slice_fusion), channel_id=1, replica_groups=mesh['energy'=32,'cuts'=16] {'energy'}, dimensions={0} | all-to-all | bytes 2097152 | tf_op jit(solution)/shard_map/all_to_all | solution.py:79
  75.7 1.1 fusion.55
  76.8 1.1 fusion.52
  77.9 1.1 convolution_add_fusion.1
  79.1 1.1 convolution_add_fusion
  80.2 0.9 fusion.1
  81.1 0.8 convolution_multiply_fusion.1
  81.9 0.8 convolution_multiply_fusion
  82.7 0.3 copy.53
  83.0 0.3 copy.54
  83.4 1.2 fusion.4
  84.5 4.9 %all-to-all-start.1 = ((bf16[128,2,8,256]{3,2,1,0:T(8,128)(2,1)}), bf16[128,2,8,256]{3,2,1,0:T(8,128)(2,1)S(1)}, u32[]{:S(2)}, u32[]{:S(2)}) async-start(bf16[128,2,8,256]{3,2,1,0:T(8,128)(2,1)} %fusion.4), calls=%async_computation.1 | async-start | bytes 2097152 | tf_op jit(solution)/shard_map/all_to_all | solution.py:85
  89.6 28.7 %all-to-all-done.1 = bf16[128,2,8,256]{3,2,1,0:T(8,128)(2,1)S(1)} async-done(((bf16[128,2,8,256]{3,2,1,0:T(8,128)(2,1)}), bf16[128,2,8,256]{3,2,1,0:T(8,128)(2,1)S(1)}, u32[]{:S(2)}, u32[]{:S(2)}) %all-to-all-start.1) | async-done | bytes 1048608 | tf_op jit(solution)/shard_map/all_to_all | solution.py:85
  118.4 0.3 fusion.23
  118.7 0.3 fusion.24
  119.0 0.3 fusion.13
  119.4 0.3 fusion.30
  119.7 0.3 fusion.14
  120.1 0.3 fusion.29
  120.4 0.3 fusion.18
  120.8 0.3 fusion.17
  121.2 1.0 copy.44
  (59 shorter events, 4.5 us)
Async XLA Ops:
  0.0 4.4 %copy-start = (bf16[1,4,2,256,256]{4,3,2,1,0:T(8,128)(2,1)S(1)}, bf16[1,4,2,256,256]{4,3,2,1,0:T(8,128)(2,1)}, u32[]{:S(2)}) copy-start(bf16[1,4,2,256,256]{4,3,2,1,0:T(8,128)(2,1)} %param.4) | copy-start | bytes 3145732
  1.4 28.0 %collective-permute-start = (bf16[1,4,2,256,256]{4,3,1,2,0:T(8,128)(2,1)S(1)}, bf16[1,4,2,256,256]{4,3,1,2,0:T(8,128)(2,1)S(1)}, u32[]{:S(2)}, u32[]{:S(2)}) collective-permute-start(bf16[1,4,2,256,256]{4,3,1,2,0:T(8,128)(2,1)S(1)} %copy.65), channel_id=1, source_target_pairs={{1,0},{2,1},{3,2},{4,3},{5,4},{6,5},{7,6},{8,7},{9,8},{10,9},{11,1... | collective-permute-start | bytes 3145736 | tf_op jit(solution)/shard_map/ppermute | solution.py:11
  5.1 1.2 %copy-start.1 = (bf16[1,4,2,256,256]{4,3,2,1,0:T(8,128)(2,1)S(1)}, bf16[1,4,2,256,256]{4,3,2,1,0:T(8,128)(2,1)}, u32[]{:S(2)}) copy-start(bf16[1,4,2,256,256]{4,3,2,1,0:T(8,128)(2,1)} %param.5) | copy-start | bytes 3145732
  83.4 6.1 %copy-start.2 = (bf16[1,4,2,256,256]{4,3,2,1,0:T(8,128)(2,1)S(1)}, bf16[1,4,2,256,256]{4,3,2,1,0:T(8,128)(2,1)}, u32[]{:S(2)}) copy-start(bf16[1,4,2,256,256]{4,3,2,1,0:T(8,128)(2,1)} %param.7) | copy-start | bytes 3145732
  84.5 33.7 %all-to-all-start.1 = ((bf16[128,2,8,256]{3,2,1,0:T(8,128)(2,1)}), bf16[128,2,8,256]{3,2,1,0:T(8,128)(2,1)S(1)}, u32[]{:S(2)}, u32[]{:S(2)}) async-start(bf16[128,2,8,256]{3,2,1,0:T(8,128)(2,1)} %fusion.4), calls=%async_computation.1 | async-start | bytes 2097152 | tf_op jit(solution)/shard_map/all_to_all | solution.py:85
